TPU v7x, 256 devices: a whole 4x4x8 slice. The times are simulated.
256 devices in a mesh: cycle: 16 (over z, core), bin: 16 (over y, x).
Axes of the slice: x: 4, y: 4, z: 8, core: 2. Of those that a mesh axis runs over, the one named last changes fastest.
Arguments:
- obs_minus_bg: bfloat16 [131072, 640], P(('cycle', 'bin')), may hold values from -30 to 30, as said below
- obs_minus_an: bfloat16 [131072, 640], P(('cycle', 'bin')), may hold values from -30 to 30, as said below
- tile_of_row: int32 [131072, 1], P(('cycle', 'bin')), may hold values from 0 to 47; in each aligned block of 512 rows (0 to 511, 512 to 1023, ...) at most 21 rows name the same one
- owner_order: int32 [48], replicated, may hold values from 0 to 47, as said below
Outputs:
- error_cov: float32 [48, 640, 640], P('bin', 'cycle')
Inputs may be any that keep to these rules, and one draw needn't show every extreme that they name: `obs_minus_bg`: each row's value lies in this range. `obs_minus_an`: each row's value lies in this range. `tile_of_row`: the rows of one device name one tile at most 21 times; some tile reaches it; every tile is named by some row. `owner_order`: a permutation of the tiles in which entry b * 3 + i is a tile of instrument i, so each index of bin owns one scan bin of each instrument.
All inputs are finite; a program needn't handle non-finite values.
Results may differ from a plain program's by a relative error of at most 0.0003.
Values may be sent and summed in bfloat16 or wider, within the bound.
A program may use at most 320 MiB of HBM per device.

v0:
```python
import jax
import jax.numpy as jnp
from jax import lax
from jax.sharding import PartitionSpec as P

C_IASI = 616
C_CRIS = 431
C_ATMS = 22


def combined_all(value, axis, join):
    pieces = jax.tree.map(lambda part: lax.all_gather(part, axis), value)
    head = jax.tree.map(lambda part: part[0], pieces)
    tail = jax.tree.map(lambda part: part[1:], pieces)
    subtotal, _ = lax.scan(lambda subtotal, piece: (join(subtotal, piece), None), head, tail)
    return subtotal


def add_tuple(left, right):
    return jax.tree.map(lambda a, b: a + b, left, right)


def make_moments(width, pieces):
    received, tile_counts = pieces
    part_bg = received[..., :width]
    part_an = received[..., width:]
    cross = jnp.einsum("skrc,skrd->kcd", part_bg, part_an, preferred_element_type=jnp.float32)
    sums = jnp.sum(received, axis=(0, 2), dtype=jnp.float32)
    number = jnp.sum(tile_counts, axis=0).astype(jnp.float32)
    return (cross, sums, number)


def on_device(obs_minus_bg, obs_minus_an, tile_of_row, owner_order):
    n_bin = lax.axis_size("bin")
    n_cycle = lax.axis_size("cycle")
    rows = tile_of_row.shape[0]
    width = obs_minus_bg.shape[1]
    tiles = owner_order.shape[0]
    per_owner = tiles // n_bin
    slot_cap = 2 * rows // tiles
    scan_bins = tiles // 3
    tile = tile_of_row[:, 0]
    instr = tile // scan_bins
    limit = jnp.where(instr == 0, C_IASI, jnp.where(instr == 1, C_CRIS, C_ATMS))
    keep = jnp.arange(width)[None, :] < limit[:, None]
    zero = jnp.zeros((), jnp.bfloat16)
    masked_bg = jnp.where(keep, obs_minus_bg, zero)
    masked_an = jnp.where(keep, obs_minus_an, zero)
    onehot = (tile[:, None] == jnp.arange(tiles)[None, :]).astype(jnp.int32)
    rank = jnp.sum((jnp.cumsum(onehot, axis=0) - 1) * onehot, axis=1)
    order_hits = (owner_order[:, None] == jnp.arange(tiles)[None, :]).astype(jnp.int32)
    position = jnp.sum(order_hits * jnp.arange(tiles, dtype=jnp.int32)[:, None], axis=0)
    row_position = jnp.sum(onehot * position[None, :], axis=1)
    counts = jnp.sum(onehot, axis=0)
    counts_owner = jnp.sum(order_hits * counts[None, :], axis=1).reshape(n_bin, per_owner)
    stacked = jnp.concatenate([masked_bg, masked_an], axis=1)
    dest = row_position * slot_cap + rank
    sendbuf = jnp.zeros((tiles * slot_cap, 2 * width), jnp.bfloat16).at[dest].set(stacked)
    sendbuf = sendbuf.reshape(n_bin, per_owner, slot_cap, 2 * width)
    cross, sums, number = make_moments(
        width,
        (
            lax.all_to_all(sendbuf, "bin", split_axis=0, concat_axis=0, tiled=True),
            lax.all_to_all(counts_owner, "bin", split_axis=0, concat_axis=0, tiled=True),
        ),
    )
    rows_c = width // n_cycle
    start = lax.axis_index("cycle") * rows_c
    cross, sums, number = combined_all((cross, sums, number), "cycle", add_tuple)
    cross_rows = lax.dynamic_slice_in_dim(cross, start, rows_c, 1)
    mean_bg = sums[:, :width] / number[:, None]
    mean_an = sums[:, width:] / number[:, None]
    mean_rows = lax.dynamic_slice_in_dim(mean_bg, start, rows_c, 1)
    return cross_rows / number[:, None, None] - mean_rows[:, :, None] * mean_an[:, None, :]


def solution(mesh):
    return jax.shard_map(
        on_device,
        mesh=mesh,
        in_specs=(
            P(("cycle", "bin"), None),
            P(("cycle", "bin"), None),
            P(("cycle", "bin"), None),
            P(),
        ),
        out_specs=P("bin", "cycle", None),
        check_vma=False,
    )
```

profile of v0, /device:TPU:1, one launch (start us, length us, event | category | flops | bytes accessed | tf_op | source)
XLA Modules:
  0.0 621.4 jit_solution(7542943708129198772)
XLA Ops:
  6.5 0.0 all-gather.6.cloned.1.call-start
  6.5 0.7 select_reduce_fusion.2
  7.3 0.7 compare_select_fusion.2
  8.0 0.7 fusion.13
  8.7 1.2 reduce-window.6
  9.9 0.2 slice_reduce_fusion
  10.1 0.9 convert_reduce_fusion.1
  11.1 2.5 fusion.9
  13.6 4.2 scatter_custom_fusion
  17.7 2.5 reshape.67
  20.2 44.2 %all_to_all.14 = bf16[16,3,21,1280]{3,2,1,0:T(8,128)(2,1)S(1)} all-to-all(bf16[16,3,21,1280]{3,2,1,0:T(8,128)(2,1)} %reshape.67), channel_id=1, replica_groups=mesh['cycle'=16,'bin'=16] {'bin'}, dimensions={0} | all-to-all | bytes 5160960 | tf_op jit(solution)/shard_map/all_to_all | solution.py:63
  64.5 0.3 fusion.14
  64.7 4.1 convolution_bitcast_fusion
  68.8 0.0 copy-start
  68.8 0.0 copy-start.1
  68.8 0.0 all-gather.6.cloned.1.call-update
  68.8 0.6 copy-done
  69.5 0.2 select_reduce_fusion.1
  69.6 0.7 all_to_all.10
  70.3 3.5 all-to-all-start.1
  73.8 0.0 copy-done.1
  73.8 0.6 dynamic-slice
  75.0 5.1 all-to-all-done.1
  80.1 0.1 convert_dynamic-update-slice_fusion
  80.2 30.5 %all-reduce = f32[48]{0:T(128)S(1)} all-reduce(f32[48]{0:T(128)S(1)} %convert_dynamic-update-slice_fusion), channel_id=4, replica_groups=mesh['cycle'=16,'bin'=16] {'cycle'}, use_global_device_ids=true, to_apply=%add | all-reduce | flops 48 | bytes 384
  110.7 0.1 slice.53
  110.8 0.1 reshape.87
  110.9 0.5 convert_reduce_fusion
  111.4 17.7 %all-gather.3 = f32[16,3,1280]{2,1,0:T(4,128)S(1)} all-gather(f32[1,3,1280]{2,1,0:T(4,128)S(1)} %bitcast.45), channel_id=3, replica_groups=mesh['cycle'=16,'bin'=16] {'cycle'}, dimensions={0}, use_global_device_ids=true | all-gather | bytes 261120 | tf_op jit(solution)/shard_map/all_gather | solution.py:12
  129.1 0.1 slice.62
  129.2 329.3 %all-gather.6.cloned.1.call-done = f32[48,640,640]{2,1,0:T(8,128)} async-done(((f32[3,640,640]{2,1,0:T(8,128)}), f32[48,640,640]{2,1,0:T(8,128)}) %all-gather.6.cloned.1.call-update) | async-done | bytes 78643216 | tf_op jit(solution)/shard_map/all_gather | solution.py:12
  458.4 5.0 slice.59
  463.4 49.3 %slice.61 = f32[45,640,640]{2,1,0:T(8,128)} slice(f32[48,640,640]{2,1,0:T(8,128)} %all-gather.6.cloned.1.call-done), slice={[3:48], [0:640], [0:640]} | slice | bytes 147456000 | tf_op jit(solution)/shard_map/slice | solution.py:14
  512.7 99.9 %while.14 = (s32[]{:T(128)}, f32[3,640,640]{2,1,0:T(8,128)}, f32[3,1280]{1,0:T(4,128)S(1)}, f32[3]{0:T(128)S(1)}, f32[15,3,640,640]{3,2,1,0:T(8,128)}, /*index=5...) while((s32[]{:T(128)}, f32[3,640,640]{2,1,0:T(8,128)}, f32[3,1280]{1,0:T(4,128)S(1)}, ...), condition=%wide.region_11.12_spmd, body=%wide.region_10.11_spmd.sunk | while | flops 1232645 | bytes 14791821 | solution.py:15
  512.7 6.6 %bitcast_add_fusion.4 = f32[3,640,640]{2,1,0:T(8,128)} fusion(f32[3,640,640]{2,1,0:T(8,128)} %get-tuple-element.122, f32[15,3,640,640]{3,2,1,0:T(8,128)} %get-tuple-element.133, s32[]{:T(128)S(6)} %copy.29), kind=kLoop, calls=%fused_computation.1.clone.1 | loop fusion | flops 1228800 | bytes 14745604 | tf_op jit(solution)/shard_map/while/body/eval_jaxpr/add | solution.py:20
  519.4 6.6 %bitcast_add_fusion.4 = f32[3,640,640]{2,1,0:T(8,128)} fusion(f32[3,640,640]{2,1,0:T(8,128)} %get-tuple-element.122, f32[15,3,640,640]{3,2,1,0:T(8,128)} %get-tuple-element.133, s32[]{:T(128)S(6)} %copy.29), kind=kLoop, calls=%fused_computation.1.clone.1 | loop fusion | flops 1228800 | bytes 14745604 | tf_op jit(solution)/shard_map/while/body/eval_jaxpr/add | solution.py:20
  526.0 6.6 %bitcast_add_fusion.4 = f32[3,640,640]{2,1,0:T(8,128)} fusion(f32[3,640,640]{2,1,0:T(8,128)} %get-tuple-element.122, f32[15,3,640,640]{3,2,1,0:T(8,128)} %get-tuple-element.133, s32[]{:T(128)S(6)} %copy.29), kind=kLoop, calls=%fused_computation.1.clone.1 | loop fusion | flops 1228800 | bytes 14745604 | tf_op jit(solution)/shard_map/while/body/eval_jaxpr/add | solution.py:20
  532.7 6.7 %bitcast_add_fusion.4 = f32[3,640,640]{2,1,0:T(8,128)} fusion(f32[3,640,640]{2,1,0:T(8,128)} %get-tuple-element.122, f32[15,3,640,640]{3,2,1,0:T(8,128)} %get-tuple-element.133, s32[]{:T(128)S(6)} %copy.29), kind=kLoop, calls=%fused_computation.1.clone.1 | loop fusion | flops 1228800 | bytes 14745604 | tf_op jit(solution)/shard_map/while/body/eval_jaxpr/add | solution.py:20
  539.4 6.6 %bitcast_add_fusion.4 = f32[3,640,640]{2,1,0:T(8,128)} fusion(f32[3,640,640]{2,1,0:T(8,128)} %get-tuple-element.122, f32[15,3,640,640]{3,2,1,0:T(8,128)} %get-tuple-element.133, s32[]{:T(128)S(6)} %copy.29), kind=kLoop, calls=%fused_computation.1.clone.1 | loop fusion | flops 1228800 | bytes 14745604 | tf_op jit(solution)/shard_map/while/body/eval_jaxpr/add | solution.py:20
  546.1 6.6 %bitcast_add_fusion.4 = f32[3,640,640]{2,1,0:T(8,128)} fusion(f32[3,640,640]{2,1,0:T(8,128)} %get-tuple-element.122, f32[15,3,640,640]{3,2,1,0:T(8,128)} %get-tuple-element.133, s32[]{:T(128)S(6)} %copy.29), kind=kLoop, calls=%fused_computation.1.clone.1 | loop fusion | flops 1228800 | bytes 14745604 | tf_op jit(solution)/shard_map/while/body/eval_jaxpr/add | solution.py:20
  552.7 6.6 %bitcast_add_fusion.4 = f32[3,640,640]{2,1,0:T(8,128)} fusion(f32[3,640,640]{2,1,0:T(8,128)} %get-tuple-element.122, f32[15,3,640,640]{3,2,1,0:T(8,128)} %get-tuple-element.133, s32[]{:T(128)S(6)} %copy.29), kind=kLoop, calls=%fused_computation.1.clone.1 | loop fusion | flops 1228800 | bytes 14745604 | tf_op jit(solution)/shard_map/while/body/eval_jaxpr/add | solution.py:20
  559.4 6.6 %bitcast_add_fusion.4 = f32[3,640,640]{2,1,0:T(8,128)} fusion(f32[3,640,640]{2,1,0:T(8,128)} %get-tuple-element.122, f32[15,3,640,640]{3,2,1,0:T(8,128)} %get-tuple-element.133, s32[]{:T(128)S(6)} %copy.29), kind=kLoop, calls=%fused_computation.1.clone.1 | loop fusion | flops 1228800 | bytes 14745604 | tf_op jit(solution)/shard_map/while/body/eval_jaxpr/add | solution.py:20
  566.0 6.6 %bitcast_add_fusion.4 = f32[3,640,640]{2,1,0:T(8,128)} fusion(f32[3,640,640]{2,1,0:T(8,128)} %get-tuple-element.122, f32[15,3,640,640]{3,2,1,0:T(8,128)} %get-tuple-element.133, s32[]{:T(128)S(6)} %copy.29), kind=kLoop, calls=%fused_computation.1.clone.1 | loop fusion | flops 1228800 | bytes 14745604 | tf_op jit(solution)/shard_map/while/body/eval_jaxpr/add | solution.py:20
  572.7 6.7 %bitcast_add_fusion.4 = f32[3,640,640]{2,1,0:T(8,128)} fusion(f32[3,640,640]{2,1,0:T(8,128)} %get-tuple-element.122, f32[15,3,640,640]{3,2,1,0:T(8,128)} %get-tuple-element.133, s32[]{:T(128)S(6)} %copy.29), kind=kLoop, calls=%fused_computation.1.clone.1 | loop fusion | flops 1228800 | bytes 14745604 | tf_op jit(solution)/shard_map/while/body/eval_jaxpr/add | solution.py:20
  579.4 6.6 %bitcast_add_fusion.4 = f32[3,640,640]{2,1,0:T(8,128)} fusion(f32[3,640,640]{2,1,0:T(8,128)} %get-tuple-element.122, f32[15,3,640,640]{3,2,1,0:T(8,128)} %get-tuple-element.133, s32[]{:T(128)S(6)} %copy.29), kind=kLoop, calls=%fused_computation.1.clone.1 | loop fusion | flops 1228800 | bytes 14745604 | tf_op jit(solution)/shard_map/while/body/eval_jaxpr/add | solution.py:20
  586.0 6.6 %bitcast_add_fusion.4 = f32[3,640,640]{2,1,0:T(8,128)} fusion(f32[3,640,640]{2,1,0:T(8,128)} %get-tuple-element.122, f32[15,3,640,640]{3,2,1,0:T(8,128)} %get-tuple-element.133, s32[]{:T(128)S(6)} %copy.29), kind=kLoop, calls=%fused_computation.1.clone.1 | loop fusion | flops 1228800 | bytes 14745604 | tf_op jit(solution)/shard_map/while/body/eval_jaxpr/add | solution.py:20
  592.7 6.6 %bitcast_add_fusion.4 = f32[3,640,640]{2,1,0:T(8,128)} fusion(f32[3,640,640]{2,1,0:T(8,128)} %get-tuple-element.122, f32[15,3,640,640]{3,2,1,0:T(8,128)} %get-tuple-element.133, s32[]{:T(128)S(6)} %copy.29), kind=kLoop, calls=%fused_computation.1.clone.1 | loop fusion | flops 1228800 | bytes 14745604 | tf_op jit(solution)/shard_map/while/body/eval_jaxpr/add | solution.py:20
  599.3 6.6 %bitcast_add_fusion.4 = f32[3,640,640]{2,1,0:T(8,128)} fusion(f32[3,640,640]{2,1,0:T(8,128)} %get-tuple-element.122, f32[15,3,640,640]{3,2,1,0:T(8,128)} %get-tuple-element.133, s32[]{:T(128)S(6)} %copy.29), kind=kLoop, calls=%fused_computation.1.clone.1 | loop fusion | flops 1228800 | bytes 14745604 | tf_op jit(solution)/shard_map/while/body/eval_jaxpr/add | solution.py:20
  606.0 6.6 %bitcast_add_fusion.4 = f32[3,640,640]{2,1,0:T(8,128)} fusion(f32[3,640,640]{2,1,0:T(8,128)} %get-tuple-element.122, f32[15,3,640,640]{3,2,1,0:T(8,128)} %get-tuple-element.133, s32[]{:T(128)S(6)} %copy.29), kind=kLoop, calls=%fused_computation.1.clone.1 | loop fusion | flops 1228800 | bytes 14745604 | tf_op jit(solution)/shard_map/while/body/eval_jaxpr/add | solution.py:20
  612.6 0.1 fusion.15
  612.7 0.1 dynamic-slice_divide_fusion
  612.8 1.8 multiply_subtract_fusion
  (37 shorter events, 0.5 us)
Async XLA Ops:
  6.5 451.9 %all-gather.6.cloned.1.call-start = ((), (), s32[]{:S(2)}) async-start(), calls=%async_computation.2 | async-start | bytes 83558400 | tf_op jit(solution)/shard_map/all_gather | solution.py:12
  68.8 0.7 copy-start
  68.8 5.0 copy-start.1
  70.3 9.7 %all-to-all-start.1 = ((s32[16,1,3]{2,1,0:T(1,128)}), s32[16,1,3]{2,1,0:T(1,128)S(1)}, u32[]{:S(2)}, u32[]{:S(2)}) async-start(s32[16,1,3]{2,1,0:T(1,128)} %bitcast.13), calls=%async_computation.1 | async-start | bytes 16384 | tf_op jit(solution)/shard_map/all_to_all | solution.py:64
Sparse Core Ops, SparseCore 0:
  69.0 389.4 all-gather.5
where the time goes:
time: 622 us; the launch traced here: 621 us
  waiting for transfers between devices  334 us (54%)
  other arithmetic  114 us (18%)
  blocking collectives  92.4 us (15%)
  local copies, waits for them, and re-layouts  59.4 us (10%)
  between operations  14.1 us (2%)
    all_gather x1, waiting for transfers between devices, combined_all(): pieces = jax.tree.map(lambda part: lax.all_gather(part, axis), value)  329 us
    add x45, other arithmetic, add_tuple(): return jax.tree.map(lambda a, b: a + b, left, right)  99.9 us
    slice x4, local copies, waits for them, and re-layouts, combined_all(): tail = jax.tree.map(lambda part: part[1:], pieces)  49.5 us
    all_to_all x1, blocking collectives, on_device(): lax.all_to_all(sendbuf, 'bin', split_axis=0, concat_axis=0, tiled=True)  44.2 us
    unnamed x1, blocking collectives  30.5 us
    all_gather x1, blocking collectives, combined_all(): pieces = jax.tree.map(lambda part: lax.all_gather(part, axis), value)  17.7 us
  transfers between devices with their start and end apart: 2, of which 2 were waited for; matrix products, arithmetic and copies ran while one was open for 0% of the time, Pallas kernels for 0%

commit v1 on v0

--- a/solution.py
+++ b/solution.py
@@ -6,18 +6,6 @@
 C_IASI = 616
 C_CRIS = 431
 C_ATMS = 22
-
-
-def combined_all(value, axis, join):
-    pieces = jax.tree.map(lambda part: lax.all_gather(part, axis), value)
-    head = jax.tree.map(lambda part: part[0], pieces)
-    tail = jax.tree.map(lambda part: part[1:], pieces)
-    subtotal, _ = lax.scan(lambda subtotal, piece: (join(subtotal, piece), None), head, tail)
-    return subtotal
-
-
-def add_tuple(left, right):
-    return jax.tree.map(lambda a, b: a + b, left, right)
 
 
 def make_moments(width, pieces):
@@ -66,13 +54,12 @@
     )
     rows_c = width // n_cycle
     start = lax.axis_index("cycle") * rows_c
-    cross, sums, number = combined_all((cross, sums, number), "cycle", add_tuple)
-    cross_rows = lax.dynamic_slice_in_dim(cross, start, rows_c, 1)
+    cross_rows = lax.psum_scatter(cross, "cycle", scatter_dimension=1, tiled=True)
+    sums, number = lax.psum((sums, number), "cycle")
     mean_bg = sums[:, :width] / number[:, None]
     mean_an = sums[:, width:] / number[:, None]
     mean_rows = lax.dynamic_slice_in_dim(mean_bg, start, rows_c, 1)
     return cross_rows / number[:, None, None] - mean_rows[:, :, None] * mean_an[:, None, :]
-
 
 def solution(mesh):
     return jax.shard_map(

time: 622 us -> 142 us (0.23)
  waiting for transfers between devices: 334 us -> 7.68 us
  other arithmetic: 114 us -> 13.6 us
  local copies, waits for them, and re-layouts: 59.4 us -> 4.3 us
    all_gather x1 -> x0, waiting for transfers between devices: 329 us -> none  [combined_all(): pieces = jax.tree.map(lambda part: lax.all_gather(part, axis), value)]
    add x45 -> x0, other arithmetic: 99.9 us -> none  [add_tuple(): return jax.tree.map(lambda a, b: a + b, left, right)]
    slice x7 -> x1, local copies, waits for them, and re-layouts: 54.7 us -> 0.23 us  [the longest x4 49.5 us: combined_all(): tail = jax.tree.map(lambda part: part[1:], pieces)]
    psum x0 -> x1, blocking collectives: none -> 48.2 us  [on_device(): sums, number = lax.psum((sums, number), 'cycle')]
    unnamed x1 -> x0, blocking collectives: 30.5 us -> none
    all_gather x1 -> x0, blocking collectives: 17.7 us -> none  [combined_all(): pieces = jax.tree.map(lambda part: lax.all_gather(part, axis), value)]
  transfers between devices with their start and end apart: 2 -> 2, of which waited for: 2 -> 2; matrix products, arithmetic and copies ran while one was open for 0% -> 1% of each run, Pallas kernels for 0% -> 0%
where the time goes in v1:
time: 142 us; the launch traced here: 139 us
  blocking collectives  92.4 us (65%)
  other arithmetic  13.6 us (10%)
  between operations  13.4 us (9%)
  waiting for transfers between devices  7.68 us (5%)
  local copies, waits for them, and re-layouts  4.3 us (3%)
  matrix products  4.04 us (3%)
  starting transfers between devices  3.47 us (2%)
    psum x1, blocking collectives, on_device(): sums, number = lax.psum((sums, number), 'cycle')  48.2 us
    all_to_all x1, blocking collectives, on_device(): lax.all_to_all(sendbuf, 'bin', split_axis=0, concat_axis=0, tiled=True)  44.2 us
    all_to_all x1, waiting for transfers between devices, on_device(): lax.all_to_all(counts_owner, 'bin', split_axis=0, concat_axis=0, tiled=True)  6.26 us
    scatter x1, other arithmetic, on_device(): jnp.zeros((tiles * slot_cap, 2 * width), jnp.bfloat16).at[dest].set(stacked)  4.17 us
    dot_general x1, matrix products, make_moments(): jnp.einsum('skrc,skrd->kcd', part_bg, part_an, preferred_element_type=jnp...  4.04 us
    all_to_all x1, starting transfers between devices, on_device(): lax.all_to_all(counts_owner, 'bin', split_axis=0, concat_axis=0, tiled=True)  3.47 us
  transfers between devices with their start and end apart: 2, of which 2 were waited for; matrix products, arithmetic and copies ran while one was open for 1% of the time, Pallas kernels for 0%

profile of v1, /device:TPU:1, one launch (start us, length us, event | category | flops | bytes accessed | tf_op | source)
XLA Modules:
  0.0 138.9 jit_solution(6469879254824244728)
XLA Ops:
  6.5 0.0 reduce-scatter.2.cloned.1.call-start
  6.5 0.7 select_reduce_fusion.2
  7.3 0.7 compare_select_fusion.2
  8.0 0.7 fusion.11
  8.7 1.2 reduce-window.6
  9.9 0.2 slice_reduce_fusion
  10.1 0.9 convert_reduce_fusion.1
  11.1 2.5 %fusion.7 = (bf16[512,640]{1,0:T(8,128)(2,1)S(1)}, bf16[512,640]{1,0:T(8,128)(2,1)}) fusion(bf16[512,640]{1,0:T(8,128)(2,1)} %param.4, s32[512]{0:T(512)S(1)} %bitcast.28, bf16[512,640]{1,0:T(8,128)(2,1)} %param.5), kind=kLoop, calls=%fused_computation.11 | loop fusion | flops 983040 | bytes 2623488 | tf_op jit(solution)/shard_map/jit(_where)/select_n | solution.py:35
  13.6 4.2 %scatter_custom_fusion = bf16[1008,1280]{1,0:T(8,128)(2,1)S(1)} fusion(s32[512]{0:T(512)S(1)} %bitcast.29, bf16[512,640]{1,0:T(8,128)(2,1)} %get-tuple-element.15, bf16[]{:T(256)} %constant.53, bf16[512,640]{1,0:T(8,128)(2,1)S(1)} %get-tuple-element.14, bf16[]{:T(256)} %constant.17.clone.1), kind=kCustom, calls=%fused_computation.5 | custom fusion | flops 2621440 | bytes 3891204 | tf_op jit(solution)/shard_map/scatter | solution.py:46
  17.7 2.5 %reshape.59 = bf16[16,3,21,1280]{3,2,1,0:T(8,128)(2,1)} reshape(bf16[1008,1280]{1,0:T(8,128)(2,1)S(1)} %scatter_custom_fusion) | data formatting | bytes 5160960 | tf_op jit(solution)/shard_map/reshape | solution.py:47
  20.2 44.2 %all_to_all.14 = bf16[16,3,21,1280]{3,2,1,0:T(8,128)(2,1)S(1)} all-to-all(bf16[16,3,21,1280]{3,2,1,0:T(8,128)(2,1)} %reshape.59), channel_id=1, replica_groups=mesh['cycle'=16,'bin'=16] {'bin'}, dimensions={0} | all-to-all | bytes 5160960 | tf_op jit(solution)/shard_map/all_to_all | solution.py:51
  64.5 0.3 fusion.12
  64.7 4.0 %convolution_bitcast_fusion = f32[3,640,640]{2,1,0:T(8,128)} fusion(bf16[16,3,21,640]{3,2,1,0:T(8,128)(2,1)S(1)} %get-tuple-element.11, bf16[16,3,21,640]{3,2,1,0:T(8,128)(2,1)S(1)} %get-tuple-element.10), kind=kOutput, calls=%fused_computation.2 | convolution fusion | flops 825753600 | bytes 7495680 | tf_op jit(solution)/shard_map/skrc,skrd->kcd/dot_general | solution.py:15
  68.7 0.0 copy-start
  68.8 0.0 reduce-scatter.2.cloned.1.call-update
  68.8 0.6 copy-done
  69.4 0.2 select_reduce_fusion.1
  69.6 0.7 all_to_all.10
  70.3 3.5 %all-to-all-start.1 = ((s32[16,1,3]{2,1,0:T(1,128)}), s32[16,1,3]{2,1,0:T(1,128)S(1)}, u32[]{:S(2)}, u32[]{:S(2)}) async-start(s32[16,1,3]{2,1,0:T(1,128)} %bitcast.8), calls=%async_computation.2 | async-start | bytes 16384 | tf_op jit(solution)/shard_map/all_to_all | solution.py:52
  73.8 6.3 %all-to-all-done.1 = s32[16,1,3]{2,1,0:T(1,128)S(1)} async-done(((s32[16,1,3]{2,1,0:T(1,128)}), s32[16,1,3]{2,1,0:T(1,128)S(1)}, u32[]{:S(2)}, u32[]{:S(2)}) %all-to-all-start.1) | async-done | bytes 224 | tf_op jit(solution)/shard_map/all_to_all | solution.py:52
  80.1 0.5 convert_reduce_fusion
  80.6 48.2 %all-reduce = (f32[3,1280]{1,0:T(4,128)S(1)}, f32[3]{0:T(128)S(1)}) all-reduce(f32[3,1280]{1,0:T(4,128)S(1)} %convert_reduce_fusion, f32[3]{0:T(128)S(1)} %convert_element_type.16), channel_id=1, replica_groups=mesh['cycle'=16,'bin'=16] {'cycle'}, use_global_device_ids=true, to_apply=%region_12.13 | all-reduce | flops 3843 | bytes 30744 | tf_op jit(solution)/shard_map/psum | solution.py:58
  128.8 0.1 fusion.13
  128.8 0.1 dynamic-slice_divide_fusion
  128.9 1.4 %reduce-scatter.2.cloned.1.call-done = f32[3,40,640]{2,1,0:T(8,128)} async-done(((f32[3,640,640]{2,1,0:T(8,128)}), f32[3,40,640]{2,1,0:T(8,128)}) %reduce-scatter.2.cloned.1.call-update) | async-done | bytes 307216 | tf_op jit(solution)/shard_map/reduce_scatter | solution.py:57
  130.3 1.8 %multiply_subtract_fusion = f32[3,40,640]{2,1,0:T(8,128)} fusion(f32[3,40,640]{2,1,0:T(8,128)} %reduce-scatter.2.cloned.1.call-done, f32[3,640]{1,0:T(4,128)S(1)} %get-tuple-element.13, f32[3,40]{1,0:T(4,128)S(1)} %dynamic-slice_divide_fusion, f32[3]{0:T(128)S(1)} %get-tuple-element.9), kind=kLoop, calls=%fused_computation.13 | loop fusion | flops 230400 | bytes 622572 | tf_op jit(solution)/shard_map/sub | solution.py:62
  (6 shorter events, 0.1 us)
Async XLA Ops:
  6.5 123.8 %reduce-scatter.2.cloned.1.call-start = ((), (), s32[]{:S(2)}) async-start(), calls=%async_computation.3 | async-start | bytes 5222400 | tf_op jit(solution)/shard_map/reduce_scatter | solution.py:57
  68.7 0.7 copy-start
  70.3 9.7 %all-to-all-start.1 = ((s32[16,1,3]{2,1,0:T(1,128)}), s32[16,1,3]{2,1,0:T(1,128)S(1)}, u32[]{:S(2)}, u32[]{:S(2)}) async-start(s32[16,1,3]{2,1,0:T(1,128)} %bitcast.8), calls=%async_computation.2 | async-start | bytes 16384 | tf_op jit(solution)/shard_map/all_to_all | solution.py:52
Sparse Core Ops, SparseCore 0:
  68.9 61.3 reduce-scatter.1
